TPU v7x, 128 devices: a whole 4x4x4 slice. The times are simulated.
128 devices in a mesh: seq: 8 (over y, core), exp: 16 (over x, z).
Axes of the slice: x: 4, y: 4, z: 4, core: 2. Of those that a mesh axis runs over, the one named last changes fastest.
Arguments:
- moe_input: bfloat16 [1024, 4096], P('seq', 'exp'), may hold values from -6 to 6
- out_grad: bfloat16 [1024, 4096], P('seq', 'exp'), may hold values from -6 to 6
- expert_ids: int32 [1024, 2], P('seq'), may hold values from 0 to 7, all different within a row; in each aligned block of 128 rows (0 to 127, 128 to 255, ...) at most 48 rows name the same one
- expert_route_weights: float32 [1024, 2], P('seq'), may hold values from 0.1 to 1
- gate_weight: bfloat16 [16, 4096, 4096], P('exp', None, 'seq'), may hold values from -0.09375 to 0.09375
- up_weight: bfloat16 [16, 4096, 4096], P('exp', None, 'seq'), may hold values from -0.09375 to 0.09375
- down_weight: bfloat16 [16, 4096, 4096], P('exp', 'seq'), may hold values from -0.0625 to 0.0625
- out_weight: bfloat16 [8192, 4096], P(None, 'exp'), may hold values from -0.09375 to 0.09375
- scan_input: bfloat16 [8192, 1024], P('exp', 'seq'), may hold values from -6 to 6
- delta_raw: bfloat16 [8192, 1024], P('exp', 'seq'), may hold values from -1 to 1024
- mixer_gate_branch: bfloat16 [8192, 1024], P('exp', 'seq'), may hold values from -6 to 6
- state_input: float32 [16, 1024], P(None, 'seq'), may hold values from -0.25 to 0.25
- state_output: float32 [16, 1024], P(None, 'seq'), may hold values from -1.5 to 1.5
- log_rates: float32 [16, 8192], P(None, 'exp'), may hold values from -9 to -3
- skip_gain: float32 [8192], P('exp'), may hold values from 0.5 to 1.5
- block_states: float32 [8, 16, 8192], P('seq', None, 'exp'), may hold values from -6 to 6
Outputs:
- resid_grad: bfloat16 [1024, 4096], P('seq', 'exp')
- probs_grad: float32 [1024, 2], P('seq')
- input_grad: bfloat16 [8192, 1024], P('exp', 'seq')
- delta_grad: bfloat16 [8192, 1024], P('exp', 'seq')
- gate_grad: bfloat16 [8192, 1024], P('exp', 'seq')
- rates_grad: float32 [16, 8192], P(None, 'exp')
- skip_grad: float32 [8192], P('exp')
Inputs may be any that keep to these rules, and one draw needn't show every extreme that they name: `expert_ids`: within each aligned block of 128 rows (one sequence shard) no expert is named by more than 48 rows, and in every draw some expert is named by exactly 48 rows of some block.
All inputs are finite; a program needn't handle non-finite values.
Results may differ from a plain program's by a relative error of at most 0.0052.
Values may be sent and summed in bfloat16 or wider, within the bound.
A program may use at most 128 MiB of HBM per device.

v0:
```python
import jax
import jax.numpy as jnp
from jax import lax
from jax.experimental import pallas as pl
from jax.experimental.pallas import tpu as pltpu
from jax.sharding import PartitionSpec as P

N_SEQ = 8
F32 = jnp.float32
BF16 = jnp.bfloat16
VMEM = pl.BlockSpec(memory_space=pltpu.VMEM)
SMEM = pl.BlockSpec(memory_space=pltpu.SMEM)


def shape(dims, kind=jnp.float32):
    return jax.ShapeDtypeStruct(dims, kind)


LOG2E = 1.4426950408889634
GR = 4
TT = 128
ROWS = 64


def softplus(v):
    return jnp.maximum(v, 0.0) + jnp.log1p(jnp.exp(-jnp.abs(v)))


def sigmoid(v):
    return 1.0 / (1.0 + jnp.exp(-v))


def spread(ref, g, val):
    ref[pl.ds(g, TT, stride=8), :] = val
    ref[pl.ds(GR + g, TT, stride=8), :] = val


def column(rep, t):
    return jnp.take_along_axis(rep, jnp.full((8, 128), t, jnp.int32), axis=1)


def grouped(ref, j):
    return jnp.concatenate(
        [ref[2 * j + p:2 * j + p + 1, g * 128:(g + 1) * 128] for p in range(2) for g in range(GR)], axis=0)


def doubled(ref, j):
    return jnp.concatenate(
        [jnp.broadcast_to(ref[2 * j + p:2 * j + p + 1, :], (GR, 128)) for p in range(2)], axis=0)


def octet(j):
    return slice(8 * j, 8 * j + 8)


def at_token(t):
    return pl.ds(pl.multiple_of(t * 8, 8), 8)


def at_state(t, j):
    return pl.ds(pl.multiple_of(t * ROWS, ROWS) + 8 * j, 8)


class Forward:
    def __init__(self, u, d, b, c, lr, st, sk, rate, decay, skip, a, ear, bb, cb, dt, us, so):
        self.__dict__.update(locals())

    def open(self):
        for g in range(GR):
            rows = pl.ds(g * 128, 128)
            spread(self.dt, g, softplus(self.d[rows, :].astype(F32).T))
            spread(self.us, g, self.u[rows, :].astype(F32).T)
        for j in range(8):
            self.rate[octet(j), :] = jnp.exp(grouped(self.lr, j))
        self.skip[...] = jnp.concatenate(
            [self.sk[0:1, g * 128:(g + 1) * 128] for p in range(2) for g in range(GR)], axis=0)
        one = jnp.ones((8, 128), F32)
        return tuple(grouped(self.st.at[0], j) for j in range(8)) + (one,) * 8

    def run(self, first, last, carry):
        rate2 = [-LOG2E * self.rate[octet(j), :] for j in range(8)]
        b_rep = [doubled(self.b, j) for j in range(8)]
        c_rep = [doubled(self.c, j) for j in range(8)]
        skip = self.skip[...]

        def step(t, carry):
            here = at_token(t)
            dt = self.dt[here, :]
            u = self.us[here, :]
            du = dt * u
            acc = jnp.zeros((8, 128), F32)
            states, products = [], []
            for j in range(8):
                spot = at_state(t, j)
                b = column(b_rep[j], t)
                c = column(c_rep[j], t)
                a = jnp.exp2(dt * rate2[j])
                state = a * carry[j] + du * b
                self.ear[spot, :] = carry[j]
                self.a[spot, :] = a
                self.bb[spot, :] = b
                self.cb[spot, :] = c
                acc = acc + c * state
                states.append(state)
                products.append(carry[8 + j] * a)
            self.so[here, :] = acc + pltpu.roll(acc, 4, 0) + skip * u
            return tuple(states + products)

        return lax.fori_loop(first, last, step, carry)

    def close(self, carry):
        for j in range(8):
            self.decay[octet(j), :] = carry[8 + j]


MESH = pl.DeviceIdType.MESH
ANY = pl.BlockSpec(memory_space=pl.ANY)
CAP = 48


def places():
    q = lax.axis_index("seq")
    e = lax.axis_index("exp")
    return q, e


def knock(peers):
    for peer in peers:
        pl.semaphore_signal(pltpu.get_barrier_semaphore(), inc=1, device_id=peer, device_id_type=MESH)


def greeted(peers):
    pl.semaphore_wait(pltpu.get_barrier_semaphore(), len(peers))


class Copies:
    def __init__(self, send, recv):
        self.send, self.recv, self.all, self.next = send, recv, [], 0

    def make(self, src, dst, peer):
        n = self.next
        self.next = n + 1
        return pltpu.make_async_remote_copy(
            src_ref=src, dst_ref=dst, send_sem=self.send.at[n], recv_sem=self.recv.at[n],
            device_id=peer, device_id_type=MESH,
        )

    def start(self, src, dst, peer):
        copy = self.make(src, dst, peer)
        copy.start()
        self.all.append(copy)
        return copy

    def finish(self):
        for copy in self.all:
            copy.wait_send()


def seq_at(y, c):
    return lax.rem(y + 4, 4) * 2 + c


def added(out, first, *others):
    total = first.astype(F32)
    for other in others:
        total = total + other.astype(F32)
    return total.astype(out)


class Ring:
    def __init__(self, cp, place, up, down, block, land):
        self.cp, self.p, self.up, self.down, self.block, self.land = cp, place, up, down, block, land

    def at(self, step, half, own=1):
        return self.block(lax.rem(self.p + step + 4, 4), half)[own]

    def far(self):
        cp, land = self.cp, self.land
        self.u2 = cp.start(self.at(2, 0, 0), land.at[0], self.up)
        self.d2 = cp.start(self.at(2, 1, 0), land.at[1], self.down)

    def near(self):
        cp, land = self.cp, self.land
        self.uh = cp.start(self.at(1, 1, 0), land.at[2], self.up)
        self.dl = cp.start(self.at(-1, 0, 0), land.at[3], self.down)

    def second(self, add):
        cp, land = self.cp, self.land
        self.u2.wait_recv()
        add(land.at[6], self.at(1, 0), land.at[0])
        self.ul = cp.start(land.at[6], land.at[4], self.up)
        self.d2.wait_recv()
        add(land.at[7], self.at(-1, 1), land.at[1])
        self.dh = cp.start(land.at[7], land.at[5], self.down)

    def last(self, add, outs):
        land = self.land
        self.dl.wait_recv()
        self.ul.wait_recv()
        add(outs[0], self.at(0, 0), land.at[4], land.at[3])
        self.uh.wait_recv()
        self.dh.wait_recv()
        add(outs[1], self.at(0, 1), land.at[2], land.at[5])


def add_rows(count):
    def add(out, *refs):
        @pl.loop(0, count)
        def _(n):
            out[n] = added(out.dtype, *[ref[n] for ref in refs])
    return add


def sems(count):
    return [pltpu.SemaphoreType.DMA((count,))] * 2


def talk(number, limit=None):
    return pltpu.CompilerParams(collective_id=number, has_side_effects=True, vmem_limit_bytes=limit)


NT = (((1,), (1,)), ((), ()))


def slots_of(ids):
    expert = lax.broadcasted_iota(jnp.int32, (8, TT), 0)
    hits = [(ids[k:k + 1, :] == expert).astype(F32) for k in range(2)]
    first = lax.broadcasted_iota(jnp.int32, (TT, TT), 0)
    second = lax.broadcasted_iota(jnp.int32, (TT, TT), 1)
    ahead = (first < second).astype(F32).astype(BF16)
    before = jnp.dot((hits[0] + hits[1]).astype(BF16), ahead, preferred_element_type=F32)
    return [jnp.sum(hit * before, axis=0, keepdims=True).astype(jnp.int32) for hit in hits]


def pack(ids_ref, x_ref, g_ref, s_ref):
    ids = ids_ref[...]
    slots = slots_of(ids)
    row = lax.broadcasted_iota(jnp.int32, (8 * CAP, TT), 0)
    hit = jnp.zeros((8 * CAP, TT), F32)
    for k in range(2):
        hit = hit + (ids[k:k + 1, :] * CAP + slots[k] == row).astype(F32)
    hot = hit.astype(BF16)
    for a, ref in enumerate((x_ref, g_ref)):
        rows = jnp.dot(hot, ref[...], preferred_element_type=F32).astype(BF16)
        for n in range(8):
            s_ref[n, a] = rows[n * CAP:(n + 1) * CAP, :]


class Arrival:
    def __init__(self, cp, arr, s, r, near):
        self.cp, self.arr, self.s, self.r, self.near = cp, arr, s, r, near
        q, e = places()
        self.q, self.e, self.h = q, e, lax.rem(e, 2)
        y, c = q // 2, lax.rem(q, 2)
        self.qu, self.qd, self.q2 = seq_at(y + 1, c), seq_at(y - 1, c), seq_at(y + 2, c)
        self.up, self.down, self.core = (self.qu, e), (self.qd, e), (y * 2 + 1 - c, e)
        self.pair = (q, e + 1 - 2 * self.h)
        self.across, self.cores = [], []

    def exchange(self):
        s, r, q, e, arr = self.s, self.r, self.q, self.e, self.arr
        x, z = e // 4, lax.rem(e, 4)

        def at(dx, dz):
            return lax.rem(x + dx, 4) * 4 + lax.rem(z + dz, 4)

        self.own = pltpu.make_async_copy(s.at[e // 2, arr], r.at[q, arr, x, z], self.near)
        self.own.start()
        self.parts = [
            self.cp.start(s.at[at(dx, dz) // 2, arr], r.at[q, arr, x, z], (q, at(dx, dz)))
            for dx in (2, 1, 3, 0) for dz in (2, 1, 3, 0) if (dx, dz) != (0, 0)]
    def move(self, shard, at, size, peer):
        ref = self.r.at[shard, self.arr, pl.ds(at, size)]
        return self.cp.start(ref, ref, peer)

    def pass_on(self, shard, at, size):
        self.cores.append(self.move(shard, at, size, self.core))

    def start(self):
        self.own.wait()
        for part in self.parts:
            part.wait_recv()
        self.a = self.move(self.q, self.h, 3, self.up)
        self.b = self.move(self.q, self.h, 3, self.down)
        self.pass_on(self.q, 0, 4)

    def middle(self):
        h = self.h
        self.a.wait_recv()
        self.f = self.move(self.qd, 2 * h, 1, self.up)
        self.across.append((self.qd, 3 - 3 * h, self.move(self.qd, 3 * h, 1, self.pair)))
        self.pass_on(self.qd, h, 3)
        self.b.wait_recv()
        self.g = self.move(self.qu, 2 * h + 1, 1, self.down)
        self.across.append((self.qu, 3 - 3 * h, self.move(self.qu, 3 * h, 1, self.pair)))
        self.pass_on(self.qu, h, 3)

    def late(self):
        h, q2 = self.h, self.q2
        self.f.wait_recv()
        self.across.append((q2, 2 - 2 * h, self.move(q2, 2 * h, 1, self.pair)))
        self.pass_on(q2, 2 * h, 1)
        self.g.wait_recv()
        self.across.append((q2, 3 - 2 * h, self.move(q2, 2 * h + 1, 1, self.pair)))
        self.pass_on(q2, 2 * h + 1, 1)
        for shard, at, copy in self.across:
            copy.wait_recv()
            self.pass_on(shard, at, 1)

    def end(self):
        for copy in self.cores:
            copy.wait_recv()


def resid_of(ids_ref, w_ref, t_ref, tp_ref, g_ref, probs_ref):
    ids = ids_ref[...]
    slots = slots_of(ids)
    weights = w_ref[...]
    table = jnp.concatenate(
        [ids[k:k + 1, :].astype(F32) for k in range(2)] + [slots[k].astype(F32) for k in range(2)]
        + [weights[k:k + 1, :] for k in range(2)] + [jnp.zeros((2, TT), F32)], axis=0).T
    lane = lax.broadcasted_iota(jnp.int32, (TT, 8 * CAP), 1)
    near = lax.broadcasted_iota(jnp.int32, (TT, 128), 1)
    total = g_ref[...].astype(F32)
    even = jnp.concatenate([t_ref[2 * n] for n in range(8)], axis=0)
    odd = jnp.concatenate([t_ref[2 * n + 1] for n in range(8)], axis=0)
    probs = []
    for k in range(2):
        name = table[:, k:k + 1].astype(jnp.int32)
        slot = table[:, 2 + k:3 + k].astype(jnp.int32)
        hot = (name * CAP + slot == lane).astype(F32).astype(BF16)
        route = jnp.dot(hot, even, preferred_element_type=F32) + jnp.dot(hot, odd, preferred_element_type=F32)
        total = total + table[:, 4 + k:5 + k] * route
        acc = jnp.zeros((TT, 128), F32)
        for n in range(8):
            row = tp_ref[2 * n, 0:1, :] + tp_ref[2 * n + 1, 0:1, :]
            acc = acc + jnp.where((name == n) & (slot == near), row, 0.0)
        probs.append(jnp.sum(acc, axis=1, keepdims=True))
    probs_ref[...] = jnp.concatenate(probs + [jnp.zeros((TT, 6), F32)], axis=1).T[:2, :]
    return total.astype(BF16)


def layer_kernel(ids_ref, w_ref, x_ref, g_ref, u, d, b_ref, c_ref, lr, st, sk, z_ref, wg_h, wu_h, wd_h, ow_h,
                 res_ref, probs_ref, gate_ref, input_ref, delta_ref, rates_ref, skipped_ref,
                 s_ref, r_ref, wg, wu, wd, gate, up, hid, dg, du, parts, pair, sums, land, final, probe, probes, mine,
                 t_ref, tp_ref, rate_ref, decay_ref, skip_ref, a, ear, bb, cb, dt, us, so,
                 ow, sent, lx, lz, kx, kz, jx, jz, inner, ys, s1s, dls,
                 term, terms, decays, part, other, both, three, send, recv, near):
    q, e = places()
    y, c = q // 2, lax.rem(q, 2)
    x, z = e // 4, lax.rem(e, 4)
    far = [(q, lax.rem(e + k, 16)) for k in range(1, 16)]
    rows = [(lax.rem(q + k, 8), e) for k in range(1, 8)]
    core = (y * 2 + 1 - c, e)
    xu, xd = (q, lax.rem(x + 1, 4) * 4 + z), (q, lax.rem(x + 3, 4) * 4 + z)
    zu, zd = (q, x * 4 + lax.rem(z + 1, 4)), (q, x * 4 + lax.rem(z + 3, 4))
    weights = [pltpu.make_async_copy(src.at[0], dst, near.at[n]) for n, (src, dst) in enumerate(
        ((wg_h, wg), (wu_h, wu), (wd_h, wd)))]
    late_load = pltpu.make_async_copy(ow_h, ow, near.at[5])
    terms[...] = jnp.zeros_like(terms)
    decays[...] = jnp.zeros_like(decays)
    knock(far + rows)
    pack(ids_ref, x_ref, g_ref, s_ref)
    for weight in weights:
        weight.start()
    late_load.start()
    greeted(far + rows)
    cp = Copies(send, recv)
    xs, gs = Arrival(cp, 0, s_ref, r_ref, near.at[3]), Arrival(cp, 1, s_ref, r_ref, near.at[4])
    xs.exchange()
    gs.exchange()
    scan = Forward(u, d, b_ref, c_ref, lr, st, sk, rate_ref, decay_ref, skip_ref, a, ear, bb, cb, dt, us, so)
    carry = scan.run(0, 40, scan.open())
    xs.start()
    scan.close(scan.run(40, TT, carry))
    xs.middle()
    gs.start()
    xs.late()
    gs.middle()
    xs.end()
    for weight in weights:
        weight.wait()

    def rows_of(arr, k):
        return jnp.concatenate([r_ref[:, arr, k, n].reshape(384, 256) for n in range(4)], axis=1)

    gate[...] = jnp.zeros_like(gate)
    up[...] = jnp.zeros_like(up)
    hid[...] = jnp.zeros_like(hid)

    @pl.loop(0, 4)
    def _(k):
        deep = pl.ds(pl.multiple_of(k * 1024, 1024), 1024)
        lhs = rows_of(0, k)
        gate[...] += jnp.dot(lhs, wg[deep, :], preferred_element_type=F32)
        up[...] += jnp.dot(lhs, wu[deep, :], preferred_element_type=F32)

    gs.late()
    gs.end()

    @pl.loop(0, 4)
    def _(k):
        deep = pl.ds(pl.multiple_of(k * 1024, 1024), 1024)
        hid[...] += lax.dot_general(rows_of(1, k), wd[:, deep], NT, preferred_element_type=F32)

    v, w, h = gate[...], up[...], hid[...]
    sig = sigmoid(v)
    dg[...] = (h * w * sig * (1.0 + v * (1.0 - sig))).astype(BF16)
    gu = h * (v * sig)
    du[...] = gu.astype(BF16)
    order = [2, 1, 3, 0]
    four = [pl.multiple_of(lax.rem(x + n, 4) * 4, 4) for n in order]
    halves, rings, shares = [], [], []

    def multiply(i):
        deep = pl.ds(pl.multiple_of(four[i] * 256, 1024), 1024)
        part = lax.dot_general(dg[...], wg[deep, :], NT, preferred_element_type=F32)
        part = part + lax.dot_general(du[...], wu[deep, :], NT, preferred_element_type=F32)
        for n in range(4):
            parts[:, :, four[i] + n] = part[:, n * 256:(n + 1) * 256].reshape(4, 2, CAP, 256).astype(BF16)
        here = pl.ds(four[i], 4)
        halves.append(cp.start(parts.at[:, 1 - c, here], pair.at[:, here], core))

    def join(i):
        halves[i].wait_recv()

        @pl.loop(0, 16)
        def _(n):
            j, m = n // 4, four[i] + lax.rem(n, 4)
            sums[j, m] = added(BF16, parts[j, c, m], pair[j, m])

        ring = Ring(cp, y, (seq_at(y + 1, c), e), (seq_at(y - 1, c), e),
                    lambda d, half: (sums.at[d, pl.ds(four[i] + 2 * half, 2)],) * 2, land.at[i])
        ring.far()
        ring.near()
        rings.append(ring)

    two = add_rows(2)

    def leave(i):
        rings[i].last(two, (final.at[pl.ds(four[i], 2)], final.at[pl.ds(four[i] + 2, 2)]))
        for m in range(4):
            to = four[i] + lax.rem(z + m, 4)
            if order[i] == 0 and m == 0:
                own = pltpu.make_async_copy(final.at[to], t_ref.at[e], near.at[6])
                own.start()
                leave.own = own
            else:
                shares.append(cp.start(final.at[to], t_ref.at[e], (q, to)))

    multiply(0)
    held = gu * w
    held = held[:, :128] + held[:, 128:256] + held[:, 256:384] + held[:, 384:]
    probe[...] = jnp.broadcast_to(jnp.sum(held.T, axis=0, keepdims=True), (8, 384))
    tells = [cp.start(probe, probes.at[k], rows[k]) for k in range(7)]
    multiply(1)
    join(0)
    multiply(2)
    join(1)
    rings[0].second(two)
    multiply(3)
    join(2)
    rings[1].second(two)
    leave(0)
    join(3)
    rings[2].second(two)
    leave(1)
    for tell in tells:
        tell.wait_recv()
    total = probe[...]
    for k in range(7):
        total = total + probes[k]
    mine[...] = pltpu.roll(total, lax.rem(8 - q, 8) * CAP, 1)[:, :128]
    rings[3].second(two)
    own_probe = pltpu.make_async_copy(mine, tp_ref.at[e], near.at[7])
    own_probe.start()
    shares += [cp.start(mine, tp_ref.at[e], peer) for peer in far]
    leave(2)
    leave(3)
    own_probe.wait()
    leave.own.wait()
    for share in shares:
        share.wait_recv()

    def earlier_shards(src, land):
        copies = []
        for k in range(1, 8):
            copy = cp.make(src, land.at[k - 1], (lax.rem(q + 8 - k, 8), e))

            @pl.when(q >= k)
            def _(copy=copy):
                copy.start()
            copies.append(copy)

        def arrive():
            for k in range(1, 8):
                @pl.when(q + k < 8)
                def _(k=k):
                    copies[k - 1].wait_recv()

        def leave():
            for k in range(1, 8):
                @pl.when(q >= k)
                def _(k=k):
                    copies[k - 1].wait_send()
        return arrive, leave

    late_load.wait()
    res_ref[...] = resid_of(ids_ref, w_ref, t_ref, tp_ref, g_ref, probs_ref)
    resid = res_ref[...]

    def inner_part(d):
        for n in range(4):
            rows = pl.ds(pl.multiple_of(d * 2048, 2048) + 512 * n, 512)
            sent[d, n] = lax.dot_general(ow[rows, :], resid, NT, preferred_element_type=F32).astype(BF16)

    def x_block(i):
        def block(d, half):
            return (sent.at[d, pl.ds(2 * half, 2), pl.ds(128 * i, 128)],) * 2
        return block

    def z_block(i):
        def block(d, half):
            return (sent.at[pl.ds(2 * half, 2), d, pl.ds(256 + 128 * i, 128)],) * 2
        return block

    def then(ref):
        def block(d, half):
            return (ref.at[d, pl.ds(64 * half, 64)],) * 2
        return block

    def one(out, *refs):
        out[...] = added(out.dtype, *[ref[...] for ref in refs])

    rx = [Ring(cp, x, xu, xd, x_block(i), lx.at[i]) for i in range(2)]
    rz = [Ring(cp, z, zu, zd, z_block(i), lz.at[i]) for i in range(2)]
    sx = [Ring(cp, z, zu, zd, then(jx.at[i]), kx.at[i]) for i in range(2)]
    sz = [Ring(cp, x, xu, xd, then(jz.at[i]), kz.at[i]) for i in range(2)]
    inner_part(lax.rem(x + 2, 4))
    for ring in rx:
        ring.far()
    inner_part(lax.rem(x + 1, 4))
    inner_part(lax.rem(x + 3, 4))
    inner_part(x)
    for ring in rz:
        ring.far()
    for ring in rx + rz:
        ring.near()
    decays_in, decays_out = earlier_shards(decay_ref, decays)
    for i in range(2):
        rx[i].second(two)
        rz[i].second(two)
    for i in range(2):
        rx[i].last(two, (jx.at[i, pl.ds(0, 2)], jx.at[i, pl.ds(2, 2)]))
        sx[i].far()
        rz[i].last(two, (jz.at[i, pl.ds(0, 2)], jz.at[i, pl.ds(2, 2)]))
        sz[i].far()
        sx[i].near()
        sz[i].near()
    for i in range(2):
        sx[i].second(one)
        sz[i].second(one)
    for i in range(2):
        sx[i].last(one, (inner.at[pl.ds(128 * i, 64)], inner.at[pl.ds(128 * i + 64, 64)]))
        sz[i].last(one, (inner.at[pl.ds(256 + 128 * i, 64)], inner.at[pl.ds(320 + 128 * i, 64)]))

    for g in range(GR):
        rows = pl.ds(g * 128, 128)
        act = z_ref[rows, :].astype(F32)
        spread(ys, g, (inner[rows, :] * act * sigmoid(act)).T)

    zero = jnp.zeros((8, 128), F32)

    def summary(i, carry):
        t = TT - 1 - i
        grad = ys[at_token(t), :]
        return tuple(a[at_state(t, j), :] * (cb[at_state(t, j), :] * grad + carry[j]) for j in range(8))

    last = lax.fori_loop(0, TT, summary, (zero,) * 8, unroll=4)
    for j in range(8):
        term[octet(j), :] = last[j]
    terms_in, terms_out = earlier_shards(term, terms)

    for g in range(GR):
        rows = pl.ds(g * 128, 128)
        act = z_ref[rows, :].astype(F32)
        sig = sigmoid(act)
        gated = inner[rows, :] * so[pl.ds(g, TT, stride=8), :].T * sig * (1.0 + act * (1.0 - sig))
        gate_ref[rows, :] = gated.astype(BF16)

    decays_in()
    terms_in()
    rate = [rate_ref[octet(j), :] for j in range(8)]
    start = []
    for j in range(8):
        inc = zero
        for k in range(7, 0, -1):
            inc = terms[k - 1, octet(j), :] + decays[k - 1, octet(j), :] * inc
        start.append(inc)

    def step(i, carry):
        vs, sums, sk = carry
        t = TT - 1 - i
        here = at_token(t)
        grad = ys[here, :]
        size = dt[here, :]
        s1, dl = zero, zero
        nv, ns = [], []
        for j in range(8):
            spot = at_state(t, j)
            adj = cb[spot, :] * grad + vs[j]
            v = a[spot, :] * adj
            w = v * ear[spot, :]
            s1 = s1 + adj * bb[spot, :]
            dl = dl + rate[j] * w
            ns.append(sums[j] + size * w)
            nv.append(v)
        s1s[here, :] = s1 + pltpu.roll(s1, 4, 0)
        dls[here, :] = dl + pltpu.roll(dl, 4, 0)
        return tuple(nv), tuple(ns), sk + grad * us[here, :]

    vs, sums, sk = lax.fori_loop(0, TT, step, (tuple(start), (zero,) * 8, zero), unroll=2)
    for j in range(8):
        part[octet(j), :] = -rate[j] * sums[j]
    part[64:72, :] = sk
    swap = cp.start(part, other, (y * 2 + 1 - c, e))

    for g in range(GR):
        rows = pl.ds(g * 128, 128)
        mine = pl.ds(g, TT, stride=8)
        s1 = s1s[mine, :]
        inp = s1 * dt[mine, :] + skip_ref[g:g + 1, :] * ys[mine, :]
        input_ref[rows, :] = inp.T.astype(BF16)

    swap.wait_recv()
    both[...] = part[...] + other[...]
    shares = [cp.start(both, three.at[k - 1], (seq_at(y + k, c), e)) for k in range(1, 4)]

    for g in range(GR):
        rows = pl.ds(g * 128, 128)
        mine = pl.ds(g, TT, stride=8)
        step_grad = us[mine, :] * s1s[mine, :] - dls[mine, :]
        delta_ref[rows, :] = (step_grad.T * sigmoid(d[rows, :].astype(F32))).astype(BF16)

    for share in shares:
        share.wait_recv()
    both2 = both[...] + three[0] + three[1] + three[2]
    for j in range(8):
        for p in range(2):
            for g in range(GR):
                row = 8 * j + GR * p + g
                rates_ref[2 * j + p:2 * j + p + 1, g * 128:(g + 1) * 128] = both2[row:row + 1, :]
    for g in range(GR):
        skipped_ref[0:1, g * 128:(g + 1) * 128] = both2[64 + g:65 + g, :]
    decays_out()
    terms_out()
    cp.finish()


def finish_kernel(*refs):
    for src, dst in zip(refs[:7], refs[7:]):
        dst[...] = src[...]


def local(
    moe_input,
    out_grad,
    expert_ids,
    expert_route_weights,
    gate_weight,
    up_weight,
    down_weight,
    out_weight,
    scan_input,
    delta_raw,
    mixer_gate_branch,
    state_input,
    state_output,
    log_rates,
    skip_gain,
    block_states,
):
    block = pltpu.VMEM((4, 16, CAP, 256), BF16)
    results = pl.pallas_call(
        layer_kernel,
        out_shape=(shape((TT, 256), BF16), shape((2, TT))) + (shape((512, 128), BF16),) * 3
        + (shape((16, 512)), shape((1, 512))),
        in_specs=[VMEM] * 12 + [ANY] * 4,
        out_specs=(VMEM,) * 7,
        scratch_shapes=[
            pltpu.VMEM((8, 2, CAP, 256), BF16),
            pltpu.VMEM((8, 2, 4, 4, CAP, 256), BF16),
            pltpu.VMEM((4096, 512), BF16),
            pltpu.VMEM((4096, 512), BF16),
            pltpu.VMEM((512, 4096), BF16),
        ] + [pltpu.VMEM((384, 512), F32)] * 3 + [pltpu.VMEM((384, 512), BF16)] * 2
        + [pltpu.VMEM((4, 2, 16, CAP, 256), BF16), block, block, pltpu.VMEM((4, 8, 2, CAP, 256), BF16),
           pltpu.VMEM((16, CAP, 256), BF16), pltpu.VMEM((8, 384), F32), pltpu.VMEM((7, 8, 384), F32),
           pltpu.VMEM((8, 128), F32), pltpu.VMEM((16, CAP, 256), BF16), pltpu.VMEM((16, 8, 128), F32)]
        + [pltpu.VMEM((ROWS, 128), F32)] * 2 + [pltpu.VMEM((8, 128), F32)]
        + [pltpu.VMEM((TT * ROWS, 128), F32)] * 4 + [pltpu.VMEM((TT * 8, 128), F32)] * 3
        + [pltpu.VMEM((8192, 256), BF16), pltpu.VMEM((4, 4, 512, TT), BF16)]
        + [pltpu.VMEM((2, 8, 2, 128, TT), BF16)] * 2 + [pltpu.VMEM((2, 8, 64, TT), F32)] * 2
        + [pltpu.VMEM((2, 4, 128, TT), F32)] * 2 + [pltpu.VMEM((512, TT), F32)]
        + [pltpu.VMEM((TT * 8, 128), F32)] * 3
        + [pltpu.VMEM((ROWS, 128), F32)] + [pltpu.VMEM((7, ROWS, 128), F32)] * 2
        + [pltpu.VMEM((72, 128), F32)] * 3 + [pltpu.VMEM((3, 72, 128), F32)]
        + sems(195) + [pltpu.SemaphoreType.DMA((8,))],
        compiler_params=talk(1, 67043328),
        name="layer_backward",
    )(expert_ids.T, expert_route_weights.T, moe_input, out_grad, scan_input, delta_raw, state_input, state_output,
      log_rates, block_states, skip_gain.reshape(1, 512), mixer_gate_branch, gate_weight, up_weight, down_weight, out_weight)
    resid_grad, probs_grad, gate_grad, input_grad, delta_grad, rates_grad, skip_grad = pl.pallas_call(
        finish_kernel,
        out_shape=tuple(shape(r.shape, r.dtype) for r in results),
        in_specs=[VMEM] * 7,
        out_specs=(VMEM,) * 7,
        name="finish",
    )(*results)
    skip_grad = skip_grad.reshape(512)
    return (resid_grad, probs_grad.T, input_grad, delta_grad, gate_grad, rates_grad, skip_grad)


def solution(mesh):
    in_specs = (
        P("seq", "exp"),
        P("seq", "exp"),
        P("seq", None),
        P("seq", None),
        P("exp", None, "seq"),
        P("exp", None, "seq"),
        P("exp", "seq", None),
        P(None, "exp"),
        P("exp", "seq"),
        P("exp", "seq"),
        P("exp", "seq"),
        P(None, "seq"),
        P(None, "seq"),
        P(None, "exp"),
        P("exp"),
        P("seq", None, "exp"),
    )
    out_specs = (
        P("seq", "exp"),
        P("seq", None),
        P("exp", "seq"),
        P("exp", "seq"),
        P("exp", "seq"),
        P(None, "exp"),
        P("exp"),
    )
    return jax.shard_map(local, mesh=mesh, in_specs=in_specs, out_specs=out_specs, check_vma=False)
```

profile of v0, /device:TPU:1, one launch (start us, length us, event | category | flops | bytes accessed | tf_op | source)
XLA Modules:
  0.0 112.0 jit_solution(10275591742743937381)
XLA Ops:
  0.6 109.5 %layer_backward.1 = (bf16[128,256]{1,0:T(8,128)(2,1)}, f32[2,128]{1,0:T(2,128)}, bf16[512,128]{1,0:T(8,128)(2,1)}, bf16[512,128]{1,0:T(8,128)(2,1)}, bf16[512,12...) custom-call(s32[2,128]{1,0:T(2,128)} %bitcast.6, f32[2,128]{1,0:T(2,128)} %bitcast.7, bf16[128,256]{1,0:T(8,128)(2,1)} %x_ref.1, ...), custom_call_target="tpu_custom_call" | custom-call | tf_op jit(solution)/shard_map/layer_backward/pallas_call | solution.py:684
  110.1 1.9 %finish.1 = (bf16[128,256]{1,0:T(8,128)(2,1)}, f32[2,128]{1,0:T(2,128)}, bf16[512,128]{1,0:T(8,128)(2,1)}, bf16[512,128]{1,0:T(8,128)(2,1)}, bf16[512,128]{1,0:T...) custom-call(bf16[128,256]{1,0:T(8,128)(2,1)} %get-tuple-element.21.refs_0_, f32[2,128]{1,0:T(2,128)} %get-tuple-element.22.refs_1_, ...), custom_call_target="tpu_custom_call" | custom-call | tf_op jit(solution)/shard_map/finish/pallas_call | solution.py:713
where the time goes:
time: 112 us
  Pallas kernels  111 us (99%)
    pallas_call x1, Pallas kernels, local(): pl.pallas_call(layer_kernel, out_shape=(shape((TT, 256), BF16), shape((2,...  109 us

commit v1 on v0

--- a/solution.py
+++ b/solution.py
@@ -280,29 +280,50 @@
         self.own.wait()
         for part in self.parts:
             part.wait_recv()
-        self.a = self.move(self.q, self.h, 3, self.up)
-        self.b = self.move(self.q, self.h, 3, self.down)
-        self.pass_on(self.q, 0, 4)
-
-    def middle(self):
+        h, q = self.h, self.q
+        self.a = self.move(q, 2 * h, 1, self.up)
+        self.b = self.move(q, 2 * h + 1, 1, self.down)
+        self.a2 = self.move(q, 2 * h + 1, 1, self.up)
+        self.b2 = self.move(q, 2 * h, 1, self.down)
+        self.pass_on(q, 0, 4)
+
+    def cross(self, shard, at, partner_at):
+        self.across.append((shard, partner_at, self.move(shard, at, 1, self.pair)))
+
+    def relay(self):
         h = self.h
         self.a.wait_recv()
         self.f = self.move(self.qd, 2 * h, 1, self.up)
-        self.across.append((self.qd, 3 - 3 * h, self.move(self.qd, 3 * h, 1, self.pair)))
-        self.pass_on(self.qd, h, 3)
+        self.a3 = self.move(self.q, 2 - h, 1, self.up)
+        self.pass_on(self.qd, 2 * h, 1)
         self.b.wait_recv()
         self.g = self.move(self.qu, 2 * h + 1, 1, self.down)
-        self.across.append((self.qu, 3 - 3 * h, self.move(self.qu, 3 * h, 1, self.pair)))
-        self.pass_on(self.qu, h, 3)
+        self.b3 = self.move(self.q, 2 - h, 1, self.down)
+        self.pass_on(self.qu, 2 * h + 1, 1)
+
+    def middle(self):
+        h = self.h
+        self.a2.wait_recv()
+        self.cross(self.qd, 3 * h, 3 - 3 * h)
+        self.pass_on(self.qd, 2 * h + 1, 1)
+        self.b2.wait_recv()
+        self.cross(self.qu, 3 * h, 3 - 3 * h)
+        self.pass_on(self.qu, 2 * h, 1)
 
     def late(self):
         h, q2 = self.h, self.q2
         self.f.wait_recv()
-        self.across.append((q2, 2 - 2 * h, self.move(q2, 2 * h, 1, self.pair)))
+        self.cross(q2, 2 * h, 2 - 2 * h)
         self.pass_on(q2, 2 * h, 1)
         self.g.wait_recv()
-        self.across.append((q2, 3 - 2 * h, self.move(q2, 2 * h + 1, 1, self.pair)))
+        self.cross(q2, 2 * h + 1, 3 - 2 * h)
         self.pass_on(q2, 2 * h + 1, 1)
+
+    def rest(self):
+        self.a3.wait_recv()
+        self.pass_on(self.qd, 2 - self.h, 1)
+        self.b3.wait_recv()
+        self.pass_on(self.qu, 2 - self.h, 1)
         for shard, at, copy in self.across:
             copy.wait_recv()
             self.pass_on(shard, at, 1)
@@ -372,11 +393,16 @@
     scan = Forward(u, d, b_ref, c_ref, lr, st, sk, rate_ref, decay_ref, skip_ref, a, ear, bb, cb, dt, us, so)
     carry = scan.run(0, 40, scan.open())
     xs.start()
-    scan.close(scan.run(40, TT, carry))
+    carry = scan.run(40, 72, carry)
+    xs.relay()
+    gs.start()
+    carry = scan.run(72, 80, carry)
     xs.middle()
-    gs.start()
+    carry = scan.run(80, 96, carry)
     xs.late()
-    gs.middle()
+    scan.close(scan.run(96, TT, carry))
+    xs.rest()
+    gs.relay()
     xs.end()
     for weight in weights:
         weight.wait()
@@ -388,14 +414,19 @@
     up[...] = jnp.zeros_like(up)
     hid[...] = jnp.zeros_like(hid)
 
-    @pl.loop(0, 4)
-    def _(k):
-        deep = pl.ds(pl.multiple_of(k * 1024, 1024), 1024)
-        lhs = rows_of(0, k)
-        gate[...] += jnp.dot(lhs, wg[deep, :], preferred_element_type=F32)
-        up[...] += jnp.dot(lhs, wu[deep, :], preferred_element_type=F32)
-
+    def gate_and_up(first, last):
+        @pl.loop(first, last)
+        def _(k):
+            deep = pl.ds(pl.multiple_of(k * 1024, 1024), 1024)
+            lhs = rows_of(0, k)
+            gate[...] += jnp.dot(lhs, wg[deep, :], preferred_element_type=F32)
+            up[...] += jnp.dot(lhs, wu[deep, :], preferred_element_type=F32)
+
+    gs.middle()
+    gate_and_up(0, 2)
     gs.late()
+    gate_and_up(2, 4)
+    gs.rest()
     gs.end()
 
     @pl.loop(0, 4)
@@ -544,8 +575,9 @@
     inner_part(x)
     for ring in rz:
         ring.far()
-    for ring in rx + rz:
-        ring.near()
+    for i in range(2):
+        rx[i].near()
+        rz[i].near()
     decays_in, decays_out = earlier_shards(decay_ref, decays)
     for i in range(2):
         rx[i].second(two)
@@ -560,14 +592,16 @@
     for i in range(2):
         sx[i].second(one)
         sz[i].second(one)
-    for i in range(2):
-        sx[i].last(one, (inner.at[pl.ds(128 * i, 64)], inner.at[pl.ds(128 * i + 64, 64)]))
-        sz[i].last(one, (inner.at[pl.ds(256 + 128 * i, 64)], inner.at[pl.ds(320 + 128 * i, 64)]))
-
-    for g in range(GR):
+    def gradient(g):
         rows = pl.ds(g * 128, 128)
         act = z_ref[rows, :].astype(F32)
         spread(ys, g, (inner[rows, :] * act * sigmoid(act)).T)
+
+    for i in range(2):
+        sx[i].last(one, (inner.at[pl.ds(128 * i, 64)], inner.at[pl.ds(128 * i + 64, 64)]))
+        gradient(i)
+        sz[i].last(one, (inner.at[pl.ds(256 + 128 * i, 64)], inner.at[pl.ds(320 + 128 * i, 64)]))
+        gradient(2 + i)
 
     zero = jnp.zeros((8, 128), F32)
 
@@ -619,7 +653,7 @@
         dls[here, :] = dl + pltpu.roll(dl, 4, 0)
         return tuple(nv), tuple(ns), sk + grad * us[here, :]
 
-    vs, sums, sk = lax.fori_loop(0, TT, step, (tuple(start), (zero,) * 8, zero), unroll=2)
+    vs, sums, sk = lax.fori_loop(0, TT, step, (tuple(start), (zero,) * 8, zero), unroll=4)
     for j in range(8):
         part[octet(j), :] = -rate[j] * sums[j]
     part[64:72, :] = sk
@@ -705,7 +739,7 @@
         + [pltpu.VMEM((TT * 8, 128), F32)] * 3
         + [pltpu.VMEM((ROWS, 128), F32)] + [pltpu.VMEM((7, ROWS, 128), F32)] * 2
         + [pltpu.VMEM((72, 128), F32)] * 3 + [pltpu.VMEM((3, 72, 128), F32)]
-        + sems(195) + [pltpu.SemaphoreType.DMA((8,))],
+        + sems(211) + [pltpu.SemaphoreType.DMA((8,))],
         compiler_params=talk(1, 67043328),
         name="layer_backward",
     )(expert_ids.T, expert_route_weights.T, moe_input, out_grad, scan_input, delta_raw, state_input, state_output,

time: 112 us -> 109 us (0.973)
  Pallas kernels: 111 us -> 108 us
    pallas_call x1, Pallas kernels: 109 us -> 106 us  [local(): pl.pallas_call(layer_kernel, out_shape=(shape((TT, 256), BF16), shape((2,...]
where the time goes in v1:
time: 109 us
  Pallas kernels  108 us (99%)
    pallas_call x1, Pallas kernels, local(): pl.pallas_call(layer_kernel, out_shape=(shape((TT, 256), BF16), shape((2,...  106 us

profile of v1, /device:TPU:1, one launch (start us, length us, event | category | flops | bytes accessed | tf_op | source)
XLA Modules:
  0.0 108.9 jit_solution(16371985994766502893)
XLA Ops:
  0.6 106.3 %layer_backward.1 = (bf16[128,256]{1,0:T(8,128)(2,1)}, f32[2,128]{1,0:T(2,128)}, bf16[512,128]{1,0:T(8,128)(2,1)}, bf16[512,128]{1,0:T(8,128)(2,1)}, bf16[512,12...) custom-call(s32[2,128]{1,0:T(2,128)} %bitcast.6, f32[2,128]{1,0:T(2,128)} %bitcast.7, bf16[128,256]{1,0:T(8,128)(2,1)} %x_ref.1, ...), custom_call_target="tpu_custom_call" | custom-call | tf_op jit(solution)/shard_map/layer_backward/pallas_call | solution.py:718
  107.0 1.9 %finish.1 = (bf16[128,256]{1,0:T(8,128)(2,1)}, f32[2,128]{1,0:T(2,128)}, bf16[512,128]{1,0:T(8,128)(2,1)}, bf16[512,128]{1,0:T(8,128)(2,1)}, bf16[512,128]{1,0:T...) custom-call(bf16[128,256]{1,0:T(8,128)(2,1)} %get-tuple-element.21.refs_0_, f32[2,128]{1,0:T(2,128)} %get-tuple-element.22.refs_1_, ...), custom_call_target="tpu_custom_call" | custom-call | tf_op jit(solution)/shard_map/finish/pallas_call | solution.py:747
